TPU v7x, 32 devices: a whole 2x2x4 slice. The times are simulated.
32 devices in a mesh: dp: 8 (over z, x), mp: 4 (over y, core).
Axes of the slice: x: 2, y: 2, z: 4, core: 2. Of those that a mesh axis runs over, the one named last changes fastest.
Arguments:
- activations: bfloat16 [4096, 3072], P('dp', 'mp'), may hold values from -6 to 6
- out_grads: bfloat16 [4096, 6144], P('dp', 'mp'), may hold values from -0.25 to 0.25
- error: bfloat16 [8, 3072, 6144], P('dp', 'mp'), may hold values from -8 to 8
- sketch: bfloat16 [6144, 64], replicated, may hold values from -0.078125 to 0.078125
- momentum: float32 [3072, 6144], P('mp', 'dp'), may hold values from -6 to 6
Outputs:
- error_new: bfloat16 [8, 3072, 6144], P('dp', 'mp')
- momentum_new: float32 [3072, 6144], P('mp', 'dp')
- next_sketch: bfloat16 [6144, 64], replicated
All inputs are finite; a program needn't handle non-finite values.
Results may differ from a plain program's by a relative error of at most 0.0057.
Values may be sent and summed in bfloat16 or wider, within the bound.
A program may use at most 64 MiB of HBM per device.

v0:
```python
import jax
import jax.numpy as jnp
from jax import lax
from jax.sharding import PartitionSpec as P

beta_decay = 0.9


def update_momentum(momentum, basis_rows, sketch_block):
    product = lax.dot_general(
        basis_rows, sketch_block, (((1,), (1,)), ((), ())), preferred_element_type=jnp.float32
    )
    return beta_decay * momentum + product


def local(activations, out_grads, error, sketch, momentum):
    own_error = error[0]
    product = lax.dot_general(
        activations,
        lax.all_gather(out_grads, "mp", axis=1, tiled=True),
        (((0,), (0,)), ((), ())),
        preferred_element_type=jnp.float32,
    )
    accumulated = (product + own_error.astype(jnp.float32)).astype(jnp.bfloat16)
    local_left = jnp.dot(accumulated, sketch, preferred_element_type=jnp.float32)
    left_sketch = lax.psum(local_left, "dp")
    gram_local = jnp.dot(
        left_sketch.T,
        left_sketch,
        precision=lax.Precision.HIGHEST,
        preferred_element_type=jnp.float32,
    )
    gram_matrix = lax.psum(gram_local, "mp")
    factor = jnp.linalg.cholesky(gram_matrix)
    basis_rows = jax.scipy.linalg.solve_triangular(factor, left_sketch.T, lower=True).T.astype(
        jnp.bfloat16
    )
    block_width = momentum.shape[1]
    local_right = lax.dot_general(
        accumulated, basis_rows, (((0,), (0,)), ((), ())), preferred_element_type=jnp.float32
    )
    right_sketch = lax.psum(local_right, ("dp", "mp"))
    next_sketch = right_sketch.astype(jnp.bfloat16)
    sketch_part = lax.dynamic_slice_in_dim(
        next_sketch, lax.axis_index("dp") * block_width, block_width, 0
    )
    momentum_new = update_momentum(momentum, basis_rows, sketch_part)
    decoded = lax.dot_general(
        basis_rows, next_sketch, (((1,), (1,)), ((), ())), preferred_element_type=jnp.float32
    )
    error_new = (accumulated.astype(jnp.float32) - decoded / lax.axis_size("dp")).astype(
        jnp.bfloat16
    )
    return (error_new[None], momentum_new, next_sketch)


def solution(mesh):
    in_specs = (P("dp", "mp"), P("dp", "mp"), P("dp", "mp", None), P(), P("mp", "dp"))
    out_specs = (P("dp", "mp", None), P("mp", "dp"), P())
    return jax.shard_map(local, mesh=mesh, in_specs=in_specs, out_specs=out_specs, check_vma=False)
```

profile of v0, /device:TPU:0, one launch (start us, length us, event | category | flops | bytes accessed | tf_op | source)
XLA Modules:
  0.0 249.4 jit_solution(14047941913646381180)
XLA Ops:
  7.2 0.0 copy-start
  7.2 0.0 all-gather.2.cloned.1.call-start
  7.2 0.7 all-gather.2.cloned.1.call-update
  7.9 0.0 copy-start.4
  7.9 0.0 all-reduce.3.cloned.1.call-start
  8.0 50.7 %all-gather.2.cloned.1.call-done = bf16[512,6144]{1,0:T(8,128)(2,1)} async-done(((bf16[512,1536]{1,0:T(8,128)(2,1)}), bf16[512,6144]{1,0:T(8,128)(2,1)}) %all-gather.2.cloned.1.call-update) | async-done | bytes 6291472 | tf_op jit(solution)/shard_map/all_gather | solution.py:20
  58.7 0.0 copy-done
  58.7 9.6 %fusion = bf16[768,6144]{1,0:T(8,128)(2,1)S(1)} fusion(bf16[1,768,6144]{2,1,0:T(8,128)(2,1)} %param.7, bf16[512,768]{1,0:T(8,128)(2,1)S(1)} %copy-done, bf16[512,6144]{1,0:T(8,128)(2,1)} %all-gather.2.cloned.1.call-done), kind=kOutput, calls=%fused_computation.1 | convolution fusion | flops 4845993984 | bytes 25952256 | tf_op jit(solution)/shard_map/dot_general | solution.py:18
  68.3 0.0 copy-start.1
  68.3 3.7 %copy-done.1 = bf16[768,6144]{1,0:T(8,128)(2,1)} copy-done((bf16[768,6144]{1,0:T(8,128)(2,1)}, bf16[768,6144]{1,0:T(8,128)(2,1)S(1)}, u32[]{:S(2)}) %copy-start.1) | copy-done | bytes 9437208
  72.1 0.0 copy-done.4
  72.1 3.7 %fusion.7 = f32[768,64]{0,1:T(8,128)} fusion(bf16[768,6144]{1,0:T(8,128)(2,1)S(1)} %fusion, bf16[6144,64]{0,1:T(8,128)(2,1)S(1)} %copy-done.4), kind=kOutput, calls=%fused_computation.17 | convolution fusion | flops 603979776 | bytes 10420224 | tf_op jit(solution)/shard_map/dot_general | solution.py:25
  75.7 0.0 all-reduce.3.cloned.1.call-update
  75.8 70.8 %all-reduce.3.cloned.1.call-done = f32[768,64]{0,1:T(8,128)} async-done(((f32[768,64]{0,1:T(8,128)}), f32[768,64]{0,1:T(8,128)}) %all-reduce.3.cloned.1.call-update) | async-done | bytes 196624 | tf_op jit(solution)/shard_map/psum | solution.py:26
  146.6 1.3 fusion.8
  147.9 10.3 %psum.22 = f32[64,64]{0,1:T(8,128)S(1)} all-reduce(f32[64,64]{0,1:T(8,128)S(1)} %fusion.8), channel_id=1, replica_groups=mesh['dp'=8,'mp'=4] {'mp'}, use_global_device_ids=true, to_apply=%region_1.0 | all-reduce | flops 4096 | bytes 32768 | tf_op jit(solution)/shard_map/psum | solution.py:33
  158.2 0.1 copy.9
  158.3 5.8 %cholesky.16 = f32[64,64]{1,0:T(8,128)S(1)} custom-call(f32[64,64]{1,0:T(8,128)S(1)} %fusion.5), custom_call_target="Cholesky" | custom-call | tf_op jit(solution)/shard_map/jit(cholesky)/cholesky | solution.py:34
  164.2 0.6 compare_reduce_fusion
  164.8 0.7 fusion.3
  165.5 4.9 %custom-call.7 = f32[1,64,64]{1,2,0:T(8,128)S(1)} custom-call(f32[1,64,64]{2,1,0:T(8,128)S(1)} %fusion.3), custom_call_target="InvertDiagBlocksLowerTriangular" | custom-call | tf_op jit(solution)/shard_map/jit(_solve_triangular)/triangular_solve | solution.py:35
  170.4 1.3 convolution_convert_fusion
  171.7 5.4 %fusion.9 = f32[6144,64]{0,1:T(8,128)S(1)} fusion(bf16[768,64]{0,1:T(8,128)(2,1)S(1)} %convolution_convert_fusion, bf16[768,6144]{1,0:T(8,128)(2,1)} %copy-done.1), kind=kOutput, calls=%fused_computation.19 | convolution fusion | flops 603979776 | bytes 11108352 | tf_op jit(solution)/shard_map/dot_general | solution.py:39
  177.1 55.7 %all-reduce.4 = bf16[6144,64]{0,1:T(8,128)(2,1)S(1)} all-reduce(f32[6144,64]{0,1:T(8,128)S(1)} %fusion.9), channel_id=1, replica_groups=mesh['dp'=8,'mp'=4] {'dp','mp'}, use_global_device_ids=true, to_apply=%region_4.5 | all-reduce | flops 393216 | bytes 2359296 | tf_op jit(solution)/shard_map/psum | solution.py:42
  232.8 0.0 copy-start.2
  232.8 0.0 copy-start.3
  232.8 7.8 %fusion.1 = bf16[1,768,6144]{2,1,0:T(8,128)(2,1)} fusion(bf16[768,64]{0,1:T(8,128)(2,1)S(1)} %convolution_convert_fusion, bf16[6144,64]{0,1:T(8,128)(2,1)S(1)} %all-reduce.4, bf16[768,6144]{1,0:T(8,128)(2,1)} %copy-done.1), kind=kOutput, calls=%fused_computation.3 | convolution fusion | flops 622854144 | bytes 19759104 | tf_op jit(solution)/shard_map/dot_general | solution.py:48
  240.7 0.0 copy-done.2
  240.7 0.0 copy-done.3
  240.7 1.9 multiply_add_fusion
  (2 shorter events, 0.0 us)
Async XLA Ops:
  7.2 51.5 %copy-start = (bf16[512,768]{1,0:T(8,128)(2,1)S(1)}, bf16[512,768]{1,0:T(8,128)(2,1)}, u32[]{:S(2)}) copy-start(bf16[512,768]{1,0:T(8,128)(2,1)} %param.5) | copy-start | bytes 2359300
  7.2 51.5 %all-gather.2.cloned.1.call-start = ((), (), s32[]{:S(2)}) async-start(), calls=%async_computation | async-start | bytes 7864320 | tf_op jit(solution)/shard_map/all_gather | solution.py:20
  7.9 64.2 %copy-start.4 = (bf16[6144,64]{0,1:T(8,128)(2,1)S(1)}, bf16[6144,64]{0,1:T(8,128)(2,1)}, u32[]{:S(2)}) copy-start(bf16[6144,64]{0,1:T(8,128)(2,1)} %param.8) | copy-start | bytes 2359300
  7.9 138.7 %all-reduce.3.cloned.1.call-start = ((), (), s32[]{:S(2)}) async-start(), calls=%async_computation.1 | async-start | bytes 393216 | tf_op jit(solution)/shard_map/psum | solution.py:26
  68.3 3.7 %copy-start.1 = (bf16[768,6144]{1,0:T(8,128)(2,1)}, bf16[768,6144]{1,0:T(8,128)(2,1)S(1)}, u32[]{:S(2)}) copy-start(bf16[768,6144]{1,0:T(8,128)(2,1)S(1)} %fusion) | copy-start | bytes 28311556
  232.8 7.8 %copy-start.2 = (bf16[6144,64]{0,1:T(8,128)(2,1)}, bf16[6144,64]{0,1:T(8,128)(2,1)S(1)}, u32[]{:S(2)}) copy-start(bf16[6144,64]{0,1:T(8,128)(2,1)S(1)} %all-reduce.4) | copy-start | bytes 2359300
  232.8 7.8 %copy-start.3 = (f32[768,768]{1,0:T(8,128)S(1)}, f32[768,768]{1,0:T(8,128)}, u32[]{:S(2)}) copy-start(f32[768,768]{1,0:T(8,128)} %param.9) | copy-start | bytes 7077892
Sparse Core Ops, SparseCore 0:
  9.5 49.0 all-gather.1
  75.9 70.6 all-reduce.2
where the time goes:
time: 250 us; the launch traced here: 249 us
  waiting for transfers between devices  122 us (49%)
  blocking collectives  66 us (26%)
  matrix products  31.1 us (12%)
  between operations  14.2 us (6%)
  other arithmetic  12.1 us (5%)
  local copies, waits for them, and re-layouts  3.84 us (2%)
    psum x1, waiting for transfers between devices, local(): left_sketch = lax.psum(local_left, 'dp')  70.8 us
    psum x1, blocking collectives, local(): right_sketch = lax.psum(local_right, ('dp', 'mp'))  55.7 us
    all_gather x1, waiting for transfers between devices, local(): lax.all_gather(out_grads, 'mp', axis=1, tiled=True)  50.7 us
    psum x1, blocking collectives, local(): gram_matrix = lax.psum(gram_local, 'mp')  10.3 us
    dot_general x1, matrix products, local(): lax.dot_general(activations, lax.all_gather(out_grads, 'mp', axis=1, tile...  9.64 us
    dot_general x1, matrix products, local(): lax.dot_general(basis_rows, next_sketch, (((1,), (1,)), ((), ())), prefer...  7.81 us
    another operation x3, other arithmetic, local(): factor = jnp.linalg.cholesky(gram_matrix)  6.52 us
    another operation x2, other arithmetic, local(): jax.scipy.linalg.solve_triangular(factor, left_sketch.T, lower=True)  5.55 us
  transfers between devices with their start and end apart: 2, of which 2 were waited for; matrix products, arithmetic and copies ran while one was open for 0% of the time, Pallas kernels for 0%

commit v1 on v0

--- a/solution.py
+++ b/solution.py
@@ -39,7 +39,7 @@
     local_right = lax.dot_general(
         accumulated, basis_rows, (((0,), (0,)), ((), ())), preferred_element_type=jnp.float32
     )
-    right_sketch = lax.psum(local_right, ("dp", "mp"))
+    right_sketch = lax.psum(lax.psum(local_right, "mp"), "dp")
     next_sketch = right_sketch.astype(jnp.bfloat16)
     sketch_part = lax.dynamic_slice_in_dim(
         next_sketch, lax.axis_index("dp") * block_width, block_width, 0

time: 250 us -> 318 us (1.27)
  waiting for transfers between devices: 122 us -> 164 us
  blocking collectives: 66 us -> 91.3 us
    psum x0 -> x1, waiting for transfers between devices: none -> 42.2 us  [local(): right_sketch = lax.psum(lax.psum(local_right, 'mp'), 'dp')]
    psum x1, blocking collectives: 55.7 us -> 81 us  [local(): right_sketch = lax.psum(lax.psum(local_right, 'mp'), 'dp')]
  transfers between devices with their start and end apart: 2 -> 3, of which waited for: 2 -> 3; matrix products, arithmetic and copies ran while one was open for 0% -> 0% of each run, Pallas kernels for 0% -> 0%
where the time goes in v1:
time: 318 us
  waiting for transfers between devices  164 us (52%)
  blocking collectives  91.3 us (29%)
  matrix products  32.2 us (10%)
  between operations  13.9 us (4%)
  other arithmetic  12.1 us (4%)
  local copies, waits for them, and re-layouts  3.84 us (1%)
    psum x1, blocking collectives, local(): right_sketch = lax.psum(lax.psum(local_right, 'mp'), 'dp')  81 us
    psum x1, waiting for transfers between devices, local(): left_sketch = lax.psum(local_left, 'dp')  70.8 us
    all_gather x1, waiting for transfers between devices, local(): lax.all_gather(out_grads, 'mp', axis=1, tiled=True)  50.7 us
    psum x1, waiting for transfers between devices, local(): right_sketch = lax.psum(lax.psum(local_right, 'mp'), 'dp')  42.2 us
    psum x1, blocking collectives, local(): gram_matrix = lax.psum(gram_local, 'mp')  10.3 us
    dot_general x1, matrix products, local(): lax.dot_general(activations, lax.all_gather(out_grads, 'mp', axis=1, tile...  9.64 us
    dot_general x1, matrix products, local(): lax.dot_general(basis_rows, next_sketch, (((1,), (1,)), ((), ())), prefer...  7.81 us
    dot_general x1, matrix products, local(): lax.dot_general(accumulated, basis_rows, (((0,), (0,)), ((), ())), prefer...  6.58 us
  transfers between devices with their start and end apart: 3, of which 3 were waited for; matrix products, arithmetic and copies ran while one was open for 0% of the time, Pallas kernels for 0%

profile of v1, /device:TPU:0, one launch (start us, length us, event | category | flops | bytes accessed | tf_op | source)
XLA Modules:
  0.0 317.8 jit_solution(17936509633370515472)
XLA Ops:
  7.2 0.0 copy-start
  7.2 0.0 all-gather.2.cloned.1.call-start
  7.2 0.7 all-gather.2.cloned.1.call-update
  7.9 0.0 copy-start.4
  7.9 0.0 all-reduce.4.cloned.1.call-start
  8.0 50.7 %all-gather.2.cloned.1.call-done = bf16[512,6144]{1,0:T(8,128)(2,1)} async-done(((bf16[512,1536]{1,0:T(8,128)(2,1)}), bf16[512,6144]{1,0:T(8,128)(2,1)}) %all-gather.2.cloned.1.call-update) | async-done | bytes 6291472 | tf_op jit(solution)/shard_map/all_gather | solution.py:20
  58.7 0.0 copy-done
  58.7 9.6 %fusion = bf16[768,6144]{1,0:T(8,128)(2,1)S(1)} fusion(bf16[1,768,6144]{2,1,0:T(8,128)(2,1)} %param.7, bf16[512,768]{1,0:T(8,128)(2,1)S(1)} %copy-done, bf16[512,6144]{1,0:T(8,128)(2,1)} %all-gather.2.cloned.1.call-done), kind=kOutput, calls=%fused_computation.1 | convolution fusion | flops 4845993984 | bytes 25952256 | tf_op jit(solution)/shard_map/dot_general | solution.py:18
  68.3 0.0 copy-start.1
  68.3 3.7 %copy-done.1 = bf16[768,6144]{1,0:T(8,128)(2,1)} copy-done((bf16[768,6144]{1,0:T(8,128)(2,1)}, bf16[768,6144]{1,0:T(8,128)(2,1)S(1)}, u32[]{:S(2)}) %copy-start.1) | copy-done | bytes 9437208
  72.1 0.0 copy-done.4
  72.1 3.7 %fusion.7 = f32[768,64]{0,1:T(8,128)} fusion(bf16[768,6144]{1,0:T(8,128)(2,1)S(1)} %fusion, bf16[6144,64]{0,1:T(8,128)(2,1)S(1)} %copy-done.4), kind=kOutput, calls=%fused_computation.17 | convolution fusion | flops 603979776 | bytes 10420224 | tf_op jit(solution)/shard_map/dot_general | solution.py:25
  75.7 0.0 all-reduce.4.cloned.1.call-update
  75.7 0.0 all-reduce.6.cloned.1.call-start
  75.8 70.8 %all-reduce.4.cloned.1.call-done = f32[768,64]{0,1:T(8,128)} async-done(((f32[768,64]{0,1:T(8,128)}), f32[768,64]{0,1:T(8,128)}) %all-reduce.4.cloned.1.call-update) | async-done | bytes 196624 | tf_op jit(solution)/shard_map/psum | solution.py:26
  146.6 1.3 fusion.8
  147.9 10.3 %psum.29 = f32[64,64]{0,1:T(8,128)S(1)} all-reduce(f32[64,64]{0,1:T(8,128)S(1)} %fusion.8), channel_id=1, replica_groups=mesh['dp'=8,'mp'=4] {'mp'}, use_global_device_ids=true, to_apply=%region_1.0 | all-reduce | flops 4096 | bytes 32768 | tf_op jit(solution)/shard_map/psum | solution.py:33
  158.2 0.1 copy.9
  158.3 5.8 %cholesky.16 = f32[64,64]{1,0:T(8,128)S(1)} custom-call(f32[64,64]{1,0:T(8,128)S(1)} %fusion.5), custom_call_target="Cholesky" | custom-call | tf_op jit(solution)/shard_map/jit(cholesky)/cholesky | solution.py:34
  164.2 0.6 compare_reduce_fusion
  164.8 0.7 fusion.3
  165.5 4.9 %custom-call.7 = f32[1,64,64]{1,2,0:T(8,128)S(1)} custom-call(f32[1,64,64]{2,1,0:T(8,128)S(1)} %fusion.3), custom_call_target="InvertDiagBlocksLowerTriangular" | custom-call | tf_op jit(solution)/shard_map/jit(_solve_triangular)/triangular_solve | solution.py:35
  170.4 1.3 convolution_convert_fusion
  171.7 6.6 %fusion.9 = f32[6144,64]{0,1:T(8,128)} fusion(bf16[768,64]{0,1:T(8,128)(2,1)S(1)} %convolution_convert_fusion, bf16[768,6144]{1,0:T(8,128)(2,1)} %copy-done.1), kind=kOutput, calls=%fused_computation.19 | convolution fusion | flops 603979776 | bytes 11108352 | tf_op jit(solution)/shard_map/dot_general | solution.py:39
  178.3 0.0 all-reduce.6.cloned.1.call-update
  178.3 42.2 %all-reduce.6.cloned.1.call-done = f32[6144,64]{0,1:T(8,128)} async-done(((f32[6144,64]{0,1:T(8,128)}), f32[6144,64]{0,1:T(8,128)}) %all-reduce.6.cloned.1.call-update) | async-done | bytes 1572880 | tf_op jit(solution)/shard_map/psum | solution.py:42
  220.5 81.0 %all-reduce.7 = bf16[6144,64]{0,1:T(8,128)(2,1)S(1)} all-reduce(f32[6144,64]{0,1:T(8,128)} %all-reduce.6.cloned.1.call-done), channel_id=1, replica_groups=mesh['dp'=8,'mp'=4] {'dp'}, use_global_device_ids=true, to_apply=%region_5.6 | all-reduce | flops 393216 | bytes 2359296 | tf_op jit(solution)/shard_map/psum | solution.py:42
  301.5 0.0 copy-start.2
  301.5 0.0 copy-start.3
  301.5 7.8 %fusion.1 = bf16[1,768,6144]{2,1,0:T(8,128)(2,1)} fusion(bf16[768,64]{0,1:T(8,128)(2,1)S(1)} %convolution_convert_fusion, bf16[6144,64]{0,1:T(8,128)(2,1)S(1)} %all-reduce.7, bf16[768,6144]{1,0:T(8,128)(2,1)} %copy-done.1), kind=kOutput, calls=%fused_computation.3 | convolution fusion | flops 622854144 | bytes 19759104 | tf_op jit(solution)/shard_map/dot_general | solution.py:48
  309.3 0.0 copy-done.2
  309.3 0.0 copy-done.3
  309.3 1.9 multiply_add_fusion
  (2 shorter events, 0.0 us)
Async XLA Ops:
  7.2 51.5 %copy-start = (bf16[512,768]{1,0:T(8,128)(2,1)S(1)}, bf16[512,768]{1,0:T(8,128)(2,1)}, u32[]{:S(2)}) copy-start(bf16[512,768]{1,0:T(8,128)(2,1)} %param.5) | copy-start | bytes 2359300
  7.2 51.5 %all-gather.2.cloned.1.call-start = ((), (), s32[]{:S(2)}) async-start(), calls=%async_computation | async-start | bytes 7864320 | tf_op jit(solution)/shard_map/all_gather | solution.py:20
  7.9 64.2 %copy-start.4 = (bf16[6144,64]{0,1:T(8,128)(2,1)S(1)}, bf16[6144,64]{0,1:T(8,128)(2,1)}, u32[]{:S(2)}) copy-start(bf16[6144,64]{0,1:T(8,128)(2,1)} %param.8) | copy-start | bytes 2359300
  7.9 138.7 %all-reduce.4.cloned.1.call-start = ((), (), s32[]{:S(2)}) async-start(), calls=%async_computation.1 | async-start | bytes 393216 | tf_op jit(solution)/shard_map/psum | solution.py:26
  68.3 3.7 %copy-start.1 = (bf16[768,6144]{1,0:T(8,128)(2,1)}, bf16[768,6144]{1,0:T(8,128)(2,1)S(1)}, u32[]{:S(2)}) copy-start(bf16[768,6144]{1,0:T(8,128)(2,1)S(1)} %fusion) | copy-start | bytes 28311556
  75.7 144.7 %all-reduce.6.cloned.1.call-start = ((), (), s32[]{:S(2)}) async-start(), calls=%async_computation.2 | async-start | bytes 3145728 | tf_op jit(solution)/shard_map/psum | solution.py:42
  301.5 7.8 %copy-start.2 = (bf16[6144,64]{0,1:T(8,128)(2,1)}, bf16[6144,64]{0,1:T(8,128)(2,1)S(1)}, u32[]{:S(2)}) copy-start(bf16[6144,64]{0,1:T(8,128)(2,1)S(1)} %all-reduce.7) | copy-start | bytes 2359300
  301.5 7.8 %copy-start.3 = (f32[768,768]{1,0:T(8,128)S(1)}, f32[768,768]{1,0:T(8,128)}, u32[]{:S(2)}) copy-start(f32[768,768]{1,0:T(8,128)} %param.9) | copy-start | bytes 7077892
Sparse Core Ops, SparseCore 0:
  9.5 49.0 all-gather.1
  75.9 70.6 all-reduce.3
  178.4 42.0 all-reduce.5
